TPU v7x, 128 devices: a whole 4x4x4 slice. The times are simulated.
128 devices in a mesh: pool: 32 (over x, z, core), exp: 4 (over y).
Axes of the slice: x: 4, y: 4, z: 4, core: 2. Of those that a mesh axis runs over, the one named last changes fastest.
Arguments:
- tokens: bfloat16 [512, 1024], P('pool'), as said below
- block_table: int32 [512, 128], replicated, may hold values from -1 to 4607, as said below
- lengths: int32 [512], replicated, may hold values from 1 to 16384, as said below
- k_cache: bfloat16 [4096, 128, 512], P('pool', None, 'exp'), as said below
- v_cache: bfloat16 [4096, 128, 512], P('pool', None, 'exp'), may hold values from -9 to 9
- hidden_store: bfloat16 [512, 128, 1024], P('pool'), may hold values from -6 to 6
- norm_attn: bfloat16 [1024], replicated, may hold values from 0.5 to 1.5
- w_query: bfloat16 [1024, 1024], P(None, 'exp'), as said below
- w_key: bfloat16 [1024, 512], P(None, 'exp'), may hold values from -0.1875 to 0.1875
- w_value: bfloat16 [1024, 512], P(None, 'exp'), may hold values from -0.1875 to 0.1875
- w_out: bfloat16 [1024, 1024], P('exp'), may hold values from -0.1875 to 0.1875
- norm_moe: bfloat16 [1024], replicated, may hold values from 0.5 to 1.5
- expert_ids: int32 [512, 8], P('pool'), may hold values from 0 to 31, all different within a row; in each aligned block of 16 rows (0 to 15, 16 to 31, ...) at most 8 rows name the same one
- gate_weights: float32 [512, 8], P('pool'), may hold values from 0.1 to 1
- w_gate: bfloat16 [32, 1024, 512], P('pool'), may hold values from -0.1875 to 0.1875
- w_up: bfloat16 [32, 1024, 512], P('pool'), may hold values from -0.1875 to 0.1875
- w_down: bfloat16 [32, 512, 1024], P('pool'), may hold values from -0.25 to 0.25
Outputs:
- layer_out: bfloat16 [512, 1024], P('pool', 'exp')
Inputs may be any that keep to these rules, and one draw needn't show every extreme that they name: `block_table`: every block number 0 to 4607 stands exactly once in the table; a request's blocks fill the start of its row and -1 fills the rest; each request has 1 to 128 blocks and some request has exactly 128. `lengths`: A request with n blocks has a length above (n - 1) * 128 and at most n * 128; some request has the length 16384. `expert_ids`: in the rows of one pool index no expert is named by more than 8 rows. `tokens`: entries lie within -8 to 8. `k_cache`: entries lie within -8 to 8. `w_query`: entries are of magnitude below 7 / sqrt(1024).
All inputs are finite; a program needn't handle non-finite values.
Results may differ from a plain program's by a relative error of at most 0.009.
Values may be sent and summed in bfloat16 or wider, within the bound.
No kernel may reach another device: no remote copies, remote signals or barrier semaphores. Data moves between devices by JAX's collectives and lax.ppermute only.
A program may use at most 128 MiB of HBM per device.

v0:
```python
import jax
import jax.numpy as jnp
from jax import lax
from jax.sharding import PartitionSpec as P

HEAD_SIZE = 64
NEG_FILL = -1e30
EPSILON = 1e-05
SCORE_SCALE = 0.125
HIGHEST = lax.Precision.HIGHEST


def merged(value, axis, join):
    pieces = jax.tree.map(lambda part: lax.all_gather(part, axis), value)
    head = jax.tree.map(lambda part: part[0], pieces)
    tail = jax.tree.map(lambda part: part[1:], pieces)
    so_far, _ = lax.scan(lambda so_far, piece: (join(so_far, piece), None), head, tail)
    return so_far


def rms_scale(row_vals, gain_row):
    mean_sq = jnp.mean(row_vals * row_vals, axis=-1, keepdims=True)
    return row_vals * lax.rsqrt(mean_sq + EPSILON) * gain_row


def merge_pair(first, second):
    top_a, sum_a, out_a = first
    top_b, sum_b, out_b = second
    row_top = jnp.maximum(top_a, top_b)
    weight_a = jnp.exp(top_a - row_top)
    weight_b = jnp.exp(top_b - row_top)
    spread = out_a.shape[-1] // top_a.shape[-1]
    merged_out = out_a * jnp.repeat(weight_a, spread, axis=-1) + out_b * jnp.repeat(
        weight_b, spread, axis=-1
    )
    return (row_top, sum_a * weight_a + sum_b * weight_b, merged_out)


def on_device(
    tokens,
    block_table,
    lengths,
    k_cache,
    v_cache,
    hidden_store,
    norm_attn,
    w_query,
    w_key,
    w_value,
    w_out,
    norm_moe,
    expert_ids,
    gate_weights,
    w_gate,
    w_up,
    w_down,
):
    pool_count = lax.axis_size("pool")
    exp_count = lax.axis_size("exp")
    pool_index = lax.axis_index("pool")
    exp_index = lax.axis_index("exp")
    req_dev = tokens.shape[0]
    model_width = tokens.shape[1]
    quarter = model_width // exp_count
    x_rows = tokens.astype(jnp.float32)
    normed = rms_scale(x_rows, norm_attn.astype(jnp.float32)).astype(jnp.bfloat16)
    queries = jnp.dot(normed, w_query, preferred_element_type=jnp.float32).astype(jnp.bfloat16)
    all_queries = lax.all_gather(queries, "pool", axis=0, tiled=True)
    stored_rows = hidden_store.reshape(-1, model_width)
    stored_shape = (hidden_store.shape[0], hidden_store.shape[1], w_key.shape[1])
    key_new = (
        jnp.dot(stored_rows, w_key, preferred_element_type=jnp.float32)
        .astype(jnp.bfloat16)
        .reshape(stored_shape)
    )
    value_new = (
        jnp.dot(stored_rows, w_value, preferred_element_type=jnp.float32)
        .astype(jnp.bfloat16)
        .reshape(stored_shape)
    )
    keys_here = jnp.concatenate([k_cache, key_new], axis=0)
    values_here = jnp.concatenate([v_cache, value_new], axis=0)
    slot_count, page_len, key_width = keys_here.shape
    query_width = queries.shape[1]
    kv_groups = key_width // HEAD_SIZE
    per_group = query_width // key_width
    head_count = query_width // HEAD_SIZE
    requests = block_table.shape[0]
    list_len = block_table.shape[1]
    flat_ids = block_table.reshape(-1)
    entry_index = jnp.arange(requests * list_len, dtype=jnp.int32)
    global_slot = pool_index * slot_count + jnp.arange(slot_count, dtype=jnp.int32)
    found_entry = jnp.sum(
        jnp.where(flat_ids[None, :] == global_slot[:, None], entry_index[None, :], 0), axis=1
    )
    slot_req = found_entry // list_len
    slot_block = found_entry % list_len
    member = slot_req[:, None] == jnp.arange(requests, dtype=jnp.int32)[None, :]
    member_low = member.astype(jnp.bfloat16)
    slot_queries = jnp.dot(member_low, all_queries, preferred_element_type=jnp.float32).astype(
        jnp.bfloat16
    )
    slot_length = jnp.sum(jnp.where(member, lengths[None, :], 0), axis=1)
    q_grouped = slot_queries.reshape(slot_count, kv_groups, per_group, HEAD_SIZE)
    k_grouped = keys_here.reshape(slot_count, page_len, kv_groups, HEAD_SIZE)
    v_grouped = values_here.reshape(slot_count, page_len, kv_groups, HEAD_SIZE)
    scores = (
        jnp.einsum("sgqd,stgd->sgqt", q_grouped, k_grouped, preferred_element_type=jnp.float32)
        * SCORE_SCALE
    )
    positions = slot_block[:, None] * page_len + jnp.arange(page_len, dtype=jnp.int32)[None, :]
    is_valid = (positions < slot_length[:, None])[:, None, None, :]
    masked = jnp.where(is_valid, scores, NEG_FILL)
    block_top = jnp.max(masked, axis=-1)
    weights = jnp.where(is_valid, jnp.exp(masked - block_top[..., None]), 0.0)
    block_sum = jnp.sum(weights, axis=-1)
    block_out = jnp.einsum(
        "sgqt,stgd->sgqd",
        weights.astype(jnp.bfloat16),
        v_grouped,
        preferred_element_type=jnp.float32,
    )
    slot_top = block_top.reshape(slot_count, head_count)
    slot_sum = block_sum.reshape(slot_count, head_count)
    slot_out = block_out.reshape(slot_count, query_width)
    local_top = jnp.max(jnp.where(member[:, :, None], slot_top[:, None, :], NEG_FILL), axis=0)
    own_top = jnp.max(jnp.where(member[:, :, None], local_top[None, :, :], NEG_FILL), axis=1)
    factor = jnp.exp(slot_top - own_top)
    one_hot = member.astype(jnp.float32)
    local_sum = jnp.einsum("sr,sh->rh", one_hot, slot_sum * factor, precision=HIGHEST)
    local_out = jnp.einsum(
        "sr,sc->rc", one_hot, slot_out * jnp.repeat(factor, HEAD_SIZE, axis=1), precision=HIGHEST
    )
    all_top, all_sum, all_out = merged((local_top, local_sum, local_out), "pool", merge_pair)
    row_start = pool_index * req_dev
    total_sum = lax.dynamic_slice_in_dim(all_sum, row_start, req_dev, 0)
    accum = lax.dynamic_slice_in_dim(all_out, row_start, req_dev, 0)
    attended = (accum / jnp.repeat(total_sum, HEAD_SIZE, axis=-1)).astype(jnp.bfloat16)
    projected = lax.psum(jnp.dot(attended, w_out, preferred_element_type=jnp.float32), "exp")
    mixed = x_rows + projected
    normed_moe = rms_scale(mixed, norm_moe.astype(jnp.float32)).astype(jnp.bfloat16)
    top_count = expert_ids.shape[1]
    capacity = min(req_dev, 2 * ((req_dev * top_count + pool_count - 1) // pool_count))
    route_flat = expert_ids.reshape(-1)
    expert_hit = (route_flat[:, None] == jnp.arange(pool_count, dtype=jnp.int32)[None, :]).astype(
        jnp.int32
    )
    slot_rank = jnp.sum(jnp.cumsum(expert_hit, axis=0) * expert_hit, axis=1) - 1
    slot_pos = route_flat * capacity + slot_rank
    placed = (
        slot_pos[:, None] == jnp.arange(pool_count * capacity, dtype=jnp.int32)[None, :]
    ).astype(jnp.float32)
    placed = placed.reshape(req_dev, top_count, pool_count * capacity)
    send_map = jnp.sum(placed, axis=1).astype(jnp.bfloat16)
    combine_map = jnp.einsum("tk,tkc->tc", gate_weights, placed, precision=HIGHEST)
    outgoing = jnp.einsum("tc,td->cd", send_map, normed_moe, preferred_element_type=jnp.float32)
    outgoing = outgoing.astype(jnp.bfloat16).reshape(pool_count, capacity, model_width)
    arrived = lax.all_to_all(outgoing, "pool", split_axis=0, concat_axis=0, tiled=True)
    sources = arrived.shape[0]
    slots_here = arrived.shape[1]
    row_block = arrived.reshape(-1, model_width)
    gate_act = jnp.dot(row_block, w_gate[0], preferred_element_type=jnp.float32)
    up_act = jnp.dot(row_block, w_up[0], preferred_element_type=jnp.float32)
    hidden = (jax.nn.silu(gate_act) * up_act).astype(jnp.bfloat16)
    expert_low = jnp.dot(hidden, w_down[0], preferred_element_type=jnp.float32).astype(jnp.bfloat16)
    expert_low = expert_low.reshape(sources, slots_here, model_width)
    expert_out = lax.dynamic_slice_in_dim(expert_low, exp_index * quarter, quarter, 2)
    returned = lax.all_to_all(expert_out, "pool", split_axis=0, concat_axis=0, tiled=True)
    moe_share = jnp.dot(
        combine_map,
        returned.reshape(pool_count * capacity, quarter).astype(jnp.float32),
        precision=HIGHEST,
    )
    mixed_share = lax.dynamic_slice_in_dim(mixed, exp_index * quarter, quarter, 1)
    return (mixed_share + moe_share).astype(jnp.bfloat16)


def solution(mesh):
    placed = (
        P("pool", None),
        P(),
        P(),
        P("pool", None, "exp"),
        P("pool", None, "exp"),
        P("pool", None, None),
        P(),
        P(None, "exp"),
        P(None, "exp"),
        P(None, "exp"),
        P("exp", None),
        P(),
        P("pool", None),
        P("pool", None),
        P("pool", None, None),
        P("pool", None, None),
        P("pool", None, None),
    )
    return jax.shard_map(
        on_device, mesh=mesh, in_specs=placed, out_specs=P("pool", "exp"), check_vma=False
    )
```

profile of v0, /device:TPU:1, one launch (start us, length us, event | category | flops | bytes accessed | tf_op | source)
XLA Modules:
  0.0 319.9 jit_solution(11277620771074689597)
XLA Ops:
  6.5 6.6 %select_reduce_fusion = s32[144]{0:T(256)S(1)} fusion(s32[65536]{0:T(1024)} %bitcast.87, s32[144]{0:T(256)S(1)} %iota_add_fusion), kind=kLoop, calls=%fused_computation.10 | loop fusion | flops 28311408 | bytes 263296 | tf_op jit(solution)/shard_map/reduce_sum | solution.py:93
  15.8 1.3 convolution_convert_fusion.5
  17.1 27.6 %all_gather.21 = bf16[512,256]{1,0:T(8,128)(2,1)S(1)} all-gather(bf16[16,256]{1,0:T(8,128)(2,1)S(1)} %convolution_convert_fusion.5), channel_id=1, replica_groups=mesh['pool'=32,'exp'=4] {'pool'}, dimensions={0}, use_global_device_ids=true | all-gather | bytes 270336 | tf_op jit(solution)/shard_map/all_gather | solution.py:68
  45.1 3.5 %convolution_convert_fusion.1 = bf16[2048,128]{1,0:T(8,128)(2,1)S(1)} fusion(bf16[2048,1024]{1,0:T(8,128)(2,1)} %bitcast.89, bf16[1024,128]{1,0:T(8,128)(2,1)} %param.27), kind=kOutput, calls=%fused_computation.20 | convolution fusion | flops 537133056 | bytes 4980736 | tf_op jit(solution)/shard_map/dot_general | solution.py:72
  49.6 6.4 %copy.75 = bf16[128,128,128]{1,2,0:T(8,128)(2,1)} copy(bf16[128,128,128]{2,1,0:T(8,128)(2,1)} %param.22) | data formatting | bytes 8388608 | tf_op args[3]
  56.1 3.7 %fusion.67 = (f32[144,2,2]{2,1,0:T(2,128)S(1)}, f32[144,2,2,128]{3,2,1,0:T(2,128)S(1)}) fusion(bf16[144,2,2,64]{3,2,1,0:T(2,128)(2,1)S(1)} %reshape.185, bf16[16,128,2,64]{1,3,2,0:T(8,128)(2,1)S(1)} %copy.77, bf16[128,128,2,64]{1,3,2,0:T(8,128)(2,1)} %bitcast.84, pred[144,128]{1,0:T(8,128)(4,1)S(1)} %add_compare_fusion), kind=kOutput, calls=%fused_computation.105 | convolution fusion | flops 12017088 | bytes 5107968 | tf_op jit(solution)/shard_map/sgqd,stgd->sgqt/dot_general | solution.py:108
  61.0 3.4 %convolution_convert_fusion = bf16[2048,128]{1,0:T(8,128)(2,1)S(1)} fusion(bf16[2048,1024]{1,0:T(8,128)(2,1)} %bitcast.90, bf16[1024,128]{1,0:T(8,128)(2,1)S(1)} %copy-done.6), kind=kOutput, calls=%fused_computation.19 | convolution fusion | flops 537133056 | bytes 4980736 | tf_op jit(solution)/shard_map/dot_general | solution.py:77
  65.5 6.4 %copy.80 = bf16[128,128,128]{1,2,0:T(8,128)(2,1)} copy(bf16[128,128,128]{2,1,0:T(8,128)(2,1)} %param.23) | data formatting | bytes 8388608 | tf_op args[4]
  71.9 4.8 %fusion.7 = f32[144,2,2,64]{3,2,1,0:T(2,128)S(1)} fusion(bf16[16,128,2,64]{1,3,2,0:T(8,128)(2,1)S(1)} %copy.82, bf16[128,128,2,64]{1,3,2,0:T(8,128)(2,1)} %bitcast.85, f32[144,2,2,128]{3,2,1,0:T(2,128)S(1)} %get-tuple-element.103, pred[144,128]{1,0:T(8,128)(4,1)S(1)} %add_compare_fusion, f32[144,2,2]{2,1,0:T(2,128)S(1)} %get-tuple-element.102), kind=kOutput, calls=%fused_computation.15 | convolution fusion | flops 12017664 | bytes 5181696 | tf_op jit(solution)/shard_map/sgqt,stgd->sgqd/dot_general | solution.py:117
  77.0 1.5 fusion.35
  79.9 24.3 %all-gather.1 = f32[16384,4]{0,1:T(4,128)S(1)} all-gather(f32[512,4]{0,1:T(4,128)S(1)} %fusion.36), channel_id=3, replica_groups=mesh['pool'=32,'exp'=4] {'pool'}, dimensions={0}, use_global_device_ids=true | all-gather | bytes 270336 | tf_op jit(solution)/shard_map/all_gather | solution.py:14
  104.3 22.6 %all-gather = f32[16384,4]{0,1:T(4,128)S(1)} all-gather(f32[512,4]{0,1:T(4,128)S(1)} %select_reduce_fusion.2), channel_id=2, replica_groups=mesh['pool'=32,'exp'=4] {'pool'}, dimensions={0}, use_global_device_ids=true | all-gather | bytes 270336 | tf_op jit(solution)/shard_map/all_gather | solution.py:14
  128.3 23.1 %all-gather.5.cloned.1.call-done = f32[16384,256]{1,0:T(8,128)} async-done(((f32[512,256]{1,0:T(8,128)}), f32[16384,256]{1,0:T(8,128)}) %all-gather.5.cloned.1.call-update) | async-done | bytes 16777232 | tf_op jit(solution)/shard_map/all_gather | solution.py:14
  152.7 11.1 %slice.35 = f32[15872,256]{1,0:T(8,128)} slice(f32[16384,256]{1,0:T(8,128)} %all-gather.5.cloned.1.call-done), slice={[512:16384], [0:256]} | slice | bytes 32505856 | tf_op jit(solution)/shard_map/slice | solution.py:16
  163.9 70.2 %while.14 = (s32[]{:T(128)}, f32[512,4]{0,1:T(4,128)S(1)}, f32[512,4]{0,1:T(4,128)S(1)}, f32[512,256]{0,1:T(8,128)S(1)}, f32[31,512,4]{1,2,0:T(4,128)}, /*index=...) while((s32[]{:T(128)}, f32[512,4]{0,1:T(4,128)S(1)}, f32[512,4]{0,1:T(4,128)S(1)}, ...), condition=%wide.region_8.9_spmd, body=%wide.region_7.8_spmd.sunk | while | flops 405506 | bytes 3752029 | solution.py:17
  164.7 1.1 constant_dynamic-slice_fusion.4
  166.9 1.1 constant_dynamic-slice_fusion.4
  169.2 1.1 constant_dynamic-slice_fusion.4
  171.5 1.1 constant_dynamic-slice_fusion.4
  173.7 1.1 constant_dynamic-slice_fusion.4
  176.0 1.1 constant_dynamic-slice_fusion.4
  178.2 1.1 constant_dynamic-slice_fusion.4
  180.5 1.1 constant_dynamic-slice_fusion.4
  182.8 1.1 constant_dynamic-slice_fusion.4
  185.0 1.1 constant_dynamic-slice_fusion.4
  187.3 1.1 constant_dynamic-slice_fusion.4
  189.6 1.1 constant_dynamic-slice_fusion.4
  191.8 1.1 constant_dynamic-slice_fusion.4
  194.1 1.1 constant_dynamic-slice_fusion.4
  196.4 1.1 constant_dynamic-slice_fusion.4
  198.6 1.1 constant_dynamic-slice_fusion.4
  200.9 1.1 constant_dynamic-slice_fusion.4
  203.1 1.1 constant_dynamic-slice_fusion.4
  205.4 1.1 constant_dynamic-slice_fusion.4
  207.7 1.1 constant_dynamic-slice_fusion.4
  209.9 1.1 constant_dynamic-slice_fusion.4
  212.2 1.1 constant_dynamic-slice_fusion.4
  216.7 1.1 constant_dynamic-slice_fusion.4
  225.8 1.1 constant_dynamic-slice_fusion.4
  228.0 1.1 constant_dynamic-slice_fusion.4
  235.3 37.8 %all-reduce.2.cloned.1.call-done = f32[16,1024]{1,0:T(8,128)} async-done(((f32[16,1024]{1,0:T(8,128)}), f32[16,1024]{1,0:T(8,128)}) %all-reduce.2.cloned.1.call-update) | async-done | bytes 65552 | tf_op jit(solution)/shard_map/psum | solution.py:139
  274.1 1.1 fusion.11
  275.2 9.7 %all-to-all-start = ((bf16[32,8,1024]{2,1,0:T(8,128)(2,1)}), bf16[32,8,1024]{2,1,0:T(8,128)(2,1)S(1)}, u32[]{:S(2)}, u32[]{:S(2)}) async-start(bf16[32,8,1024]{2,1,0:T(8,128)(2,1)} %fusion.11), calls=%async_computation | async-start | bytes 1048576 | tf_op jit(solution)/shard_map/all_to_all | solution.py:158
  285.0 11.5 %all-to-all-done = bf16[32,8,1024]{2,1,0:T(8,128)(2,1)S(1)} async-done(((bf16[32,8,1024]{2,1,0:T(8,128)(2,1)}), bf16[32,8,1024]{2,1,0:T(8,128)(2,1)S(1)}, u32[]{:S(2)}, u32[]{:S(2)}) %all-to-all-start) | async-done | bytes 524320 | tf_op jit(solution)/shard_map/all_to_all | solution.py:158
  296.5 1.7 fusion.20
  298.2 2.0 fusion.12
  300.9 3.6 %all-to-all-start.1 = ((bf16[32,8,256]{2,1,0:T(8,128)(2,1)}), bf16[32,8,256]{2,1,0:T(8,128)(2,1)S(1)}, u32[]{:S(2)}, u32[]{:S(2)}) async-start(bf16[32,8,256]{2,1,0:T(8,128)(2,1)} %constant_dynamic-slice_fusion.2), calls=%async_computation.1 | async-start | bytes 262144 | tf_op jit(solution)/shard_map/all_to_all | solution.py:168
  304.8 7.4 %all-to-all-done.1 = bf16[32,8,256]{2,1,0:T(8,128)(2,1)S(1)} async-done(((bf16[32,8,256]{2,1,0:T(8,128)(2,1)}), bf16[32,8,256]{2,1,0:T(8,128)(2,1)S(1)}, u32[]{:S(2)}, u32[]{:S(2)}) %all-to-all-start.1) | async-done | bytes 131104 | tf_op jit(solution)/shard_map/all_to_all | solution.py:168
  (169 shorter events, 56.9 us)
Async XLA Ops:
  6.5 291.6 %copy-start = (bf16[1,512,1024]{2,1,0:T(8,128)(2,1)S(1)}, bf16[1,512,1024]{2,1,0:T(8,128)(2,1)}, u32[]{:S(2)}) copy-start(bf16[1,512,1024]{2,1,0:T(8,128)(2,1)} %param.35) | copy-start | bytes 3145732
  6.5 144.9 %all-gather.5.cloned.1.call-start = ((), (), s32[]{:S(2)}) async-start(), calls=%async_computation.3 | async-start | bytes 17301504 | tf_op jit(solution)/shard_map/all_gather | solution.py:14
  56.1 4.9 %copy-start.6 = (bf16[1024,128]{1,0:T(8,128)(2,1)S(1)}, bf16[1024,128]{1,0:T(8,128)(2,1)}, u32[]{:S(2)}) copy-start(bf16[1024,128]{1,0:T(8,128)(2,1)} %param.28) | copy-start | bytes 786436
  76.7 50.9 %copy-start.3 = (s32[16,8]{0,1:T(8,128)S(1)}, s32[16,8]{0,1:T(8,128)}, u32[]{:S(2)}) copy-start(s32[16,8]{0,1:T(8,128)} %param.31) | copy-start | bytes 1540
  76.7 51.6 %copy-start.5 = (bf16[1024]{0:T(1024)(128)(2,1)S(1)}, bf16[1024]{0:T(1024)(128)(2,1)}, u32[]{:S(2)}) copy-start(bf16[1024]{0:T(1024)(128)(2,1)} %param.30) | copy-start | bytes 6148
  78.5 194.6 %all-reduce.2.cloned.1.call-start = ((), (), s32[]{:S(2)}) async-start(), calls=%async_computation.2 | async-start | bytes 131072 | tf_op jit(solution)/shard_map/psum | solution.py:139
  163.9 70.4 %copy-start.1 = (bf16[256,1024]{1,0:T(8,128)(2,1)S(1)}, bf16[256,1024]{1,0:T(8,128)(2,1)}, u32[]{:S(2)}) copy-start(bf16[256,1024]{1,0:T(8,128)(2,1)} %param.29) | copy-start | bytes 1572868
  163.9 109.2 %copy-start.2 = (bf16[16,1024]{1,0:T(8,128)(2,1)S(1)}, bf16[16,1024]{1,0:T(8,128)(2,1)}, u32[]{:S(2)}) copy-start(bf16[16,1024]{1,0:T(8,128)(2,1)} %param.19) | copy-start | bytes 98308
  163.9 121.0 %copy-start.4 = (f32[16,8]{0,1:T(8,128)S(1)}, f32[16,8]{0,1:T(8,128)}, u32[]{:S(2)}) copy-start(f32[16,8]{0,1:T(8,128)} %param.32) | copy-start | bytes 1540
  275.2 21.3 %all-to-all-start = ((bf16[32,8,1024]{2,1,0:T(8,128)(2,1)}), bf16[32,8,1024]{2,1,0:T(8,128)(2,1)S(1)}, u32[]{:S(2)}, u32[]{:S(2)}) async-start(bf16[32,8,1024]{2,1,0:T(8,128)(2,1)} %fusion.11), calls=%async_computation | async-start | bytes 1048576 | tf_op jit(solution)/shard_map/all_to_all | solution.py:158
  300.9 11.3 %all-to-all-start.1 = ((bf16[32,8,256]{2,1,0:T(8,128)(2,1)}), bf16[32,8,256]{2,1,0:T(8,128)(2,1)S(1)}, u32[]{:S(2)}, u32[]{:S(2)}) async-start(bf16[32,8,256]{2,1,0:T(8,128)(2,1)} %constant_dynamic-slice_fusion.2), calls=%async_computation.1 | async-start | bytes 262144 | tf_op jit(solution)/shard_map/all_to_all | solution.py:168
Sparse Core Ops, SparseCore 0:
  78.6 72.7 all-gather.4
  235.3 37.7 all-reduce.1
where the time goes:
time: 324 us; the launch traced here: 320 us
  waiting for transfers between devices  79.9 us (25%)
  blocking collectives  74.6 us (23%)
  local copies, waits for them, and re-layouts  70 us (22%)
  other arithmetic  42 us (13%)
  matrix products  25.4 us (8%)
  between operations  13.7 us (4%)
  starting transfers between devices  13.4 us (4%)
    all_gather x2, blocking collectives, merged(): pieces = jax.tree.map(lambda part: lax.all_gather(part, axis), value)  47 us
    dynamic_slice x62, local copies, waits for them, and re-layouts, merged(): lax.scan(lambda so_far, piece: (join(so_far, piece), None), head, tail)  39.6 us
    psum x1, waiting for transfers between devices, on_device(): lax.psum(jnp.dot(attended, w_out, preferred_element_type=jnp.float32), 'e...  37.8 us
    all_gather x1, blocking collectives, on_device(): all_queries = lax.all_gather(queries, 'pool', axis=0, tiled=True)  27.6 us
    all_gather x1, waiting for transfers between devices, merged(): pieces = jax.tree.map(lambda part: lax.all_gather(part, axis), value)  23.1 us
    add x31, other arithmetic, merge_pair(): return (row_top, sum_a * weight_a + sum_b * weight_b, merged_out)  22.5 us
    unnamed x18, local copies, waits for them, and re-layouts  13 us
    slice x3, local copies, waits for them, and re-layouts, merged(): tail = jax.tree.map(lambda part: part[1:], pieces)  11.9 us
  transfers between devices with their start and end apart: 4, of which 4 were waited for; matrix products, arithmetic and copies ran while one was open for 1% of the time, Pallas kernels for 0%

commit v1 on v0

--- a/solution.py
+++ b/solution.py
@@ -65,7 +65,9 @@
     x_rows = tokens.astype(jnp.float32)
     normed = rms_scale(x_rows, norm_attn.astype(jnp.float32)).astype(jnp.bfloat16)
     queries = jnp.dot(normed, w_query, preferred_element_type=jnp.float32).astype(jnp.bfloat16)
-    all_queries = lax.all_gather(queries, "pool", axis=0, tiled=True)
+    all_queries = jnp.concatenate(
+        lax.all_to_all(jnp.stack([queries] * lax.axis_size("pool")), "pool", 0, 0), axis=0
+    )
     stored_rows = hidden_store.reshape(-1, model_width)
     stored_shape = (hidden_store.shape[0], hidden_store.shape[1], w_key.shape[1])
     key_new = (

time: 324 us -> 306 us (0.944)
  blocking collectives: 74.6 us -> 49.3 us
  starting transfers between devices: 13.4 us -> 22.8 us
    all_gather x1 -> x0, blocking collectives: 27.6 us -> none  [on_device(): all_queries = lax.all_gather(queries, 'pool', axis=0, tiled=True)]
    all_to_all x0 -> x1, starting transfers between devices: none -> 9.43 us  [on_device(): lax.all_to_all(jnp.stack([queries] * lax.axis_size('pool')), 'pool', 0, 0)]
    unnamed x18 -> x22, local copies, waits for them, and re-layouts: 13 us -> 13 us
  transfers between devices with their start and end apart: 4 -> 5, of which waited for: 4 -> 4; matrix products, arithmetic and copies ran while one was open for 1% -> 10% of each run, Pallas kernels for 0% -> 0%
where the time goes in v1:
time: 306 us; the launch traced here: 302 us
  waiting for transfers between devices  79.7 us (26%)
  local copies, waits for them, and re-layouts  71.1 us (23%)
  blocking collectives  49.3 us (16%)
  other arithmetic  41.5 us (14%)
  matrix products  23.2 us (8%)
  starting transfers between devices  22.8 us (7%)
  between operations  13.8 us (5%)
    all_gather x2, blocking collectives, merged(): pieces = jax.tree.map(lambda part: lax.all_gather(part, axis), value)  49.3 us
    dynamic_slice x62, local copies, waits for them, and re-layouts, merged(): lax.scan(lambda so_far, piece: (join(so_far, piece), None), head, tail)  39.6 us
    psum x1, waiting for transfers between devices, on_device(): lax.psum(jnp.dot(attended, w_out, preferred_element_type=jnp.float32), 'e...  37.8 us
    all_gather x1, waiting for transfers between devices, merged(): pieces = jax.tree.map(lambda part: lax.all_gather(part, axis), value)  22.9 us
    add x31, other arithmetic, merge_pair(): return (row_top, sum_a * weight_a + sum_b * weight_b, merged_out)  22.5 us
    unnamed x22, local copies, waits for them, and re-layouts  13 us
    slice x3, local copies, waits for them, and re-layouts, merged(): tail = jax.tree.map(lambda part: part[1:], pieces)  12.1 us
    all_to_all x1, waiting for transfers between devices, on_device(): lax.all_to_all(outgoing, 'pool', split_axis=0, concat_axis=0, tiled=True)  11.5 us
  transfers between devices with their start and end apart: 5, of which 4 were waited for; matrix products, arithmetic and copies ran while one was open for 10% of the time, Pallas kernels for 0%

profile of v1, /device:TPU:1, one launch (start us, length us, event | category | flops | bytes accessed | tf_op | source)
XLA Modules:
  0.0 302.3 jit_solution(8689195608212112939)
XLA Ops:
  8.2 1.3 convolution_convert_fusion.5
  10.2 9.4 %all-to-all-start = ((bf16[32,16,256]{2,1,0:T(8,128)(2,1)}), bf16[32,16,256]{2,1,0:T(8,128)(2,1)S(1)}, u32[]{:S(2)}, u32[]{:S(2)}) async-start(bf16[32,16,256]{2,1,0:T(8,128)(2,1)} %stack.2), calls=%async_computation | async-start | bytes 524288 | tf_op jit(solution)/shard_map/all_to_all | solution.py:69
  19.8 6.7 %select_reduce_fusion = s32[144]{0:T(256)S(1)} fusion(s32[65536]{0:T(1024)} %bitcast.89, s32[144]{0:T(256)S(1)} %iota_add_fusion), kind=kLoop, calls=%fused_computation.10 | loop fusion | flops 28311408 | bytes 263296 | tf_op jit(solution)/shard_map/reduce_sum | solution.py:95
  26.5 3.5 %convolution_convert_fusion.1 = bf16[2048,128]{1,0:T(8,128)(2,1)S(1)} fusion(bf16[2048,1024]{1,0:T(8,128)(2,1)} %bitcast.91, bf16[1024,128]{1,0:T(8,128)(2,1)} %param.27), kind=kOutput, calls=%fused_computation.20 | convolution fusion | flops 537133056 | bytes 4980736 | tf_op jit(solution)/shard_map/dot_general | solution.py:74
  30.0 1.3 convolution_convert_fusion
  32.8 6.4 %copy.75 = bf16[128,128,128]{1,2,0:T(8,128)(2,1)} copy(bf16[128,128,128]{2,1,0:T(8,128)(2,1)} %param.22) | data formatting | bytes 8388608 | tf_op args[3]
  40.3 6.4 %copy.80 = bf16[128,128,128]{1,2,0:T(8,128)(2,1)} copy(bf16[128,128,128]{2,1,0:T(8,128)(2,1)} %param.23) | data formatting | bytes 8388608 | tf_op args[4]
  47.2 3.7 %fusion.67 = (f32[144,2,2]{2,1,0:T(2,128)S(1)}, f32[144,2,2,128]{3,2,1,0:T(2,128)S(1)}) fusion(bf16[144,2,2,64]{3,2,1,0:T(2,128)(2,1)S(1)} %reshape.191, bf16[16,128,2,64]{1,3,2,0:T(8,128)(2,1)S(1)} %copy.77, bf16[128,128,2,64]{1,3,2,0:T(8,128)(2,1)} %bitcast.86, pred[144,128]{1,0:T(8,128)(4,1)S(1)} %add_compare_fusion), kind=kOutput, calls=%fused_computation.105 | convolution fusion | flops 12017088 | bytes 5107968 | tf_op jit(solution)/shard_map/sgqd,stgd->sgqt/dot_general | solution.py:110
  52.1 4.8 %fusion.7 = f32[144,2,2,64]{3,2,1,0:T(2,128)S(1)} fusion(bf16[16,128,2,64]{1,3,2,0:T(8,128)(2,1)S(1)} %copy.82, bf16[128,128,2,64]{1,3,2,0:T(8,128)(2,1)} %bitcast.85, f32[144,2,2,128]{3,2,1,0:T(2,128)S(1)} %get-tuple-element.103, pred[144,128]{1,0:T(8,128)(4,1)S(1)} %add_compare_fusion, f32[144,2,2]{2,1,0:T(2,128)S(1)} %get-tuple-element.102), kind=kOutput, calls=%fused_computation.15 | convolution fusion | flops 12017664 | bytes 5181696 | tf_op jit(solution)/shard_map/sgqt,stgd->sgqd/dot_general | solution.py:119
  57.2 1.5 fusion.35
  60.8 25.1 %all-gather.1 = f32[16384,4]{0,1:T(4,128)S(1)} all-gather(f32[512,4]{0,1:T(4,128)S(1)} %fusion.36), channel_id=3, replica_groups=mesh['pool'=32,'exp'=4] {'pool'}, dimensions={0}, use_global_device_ids=true | all-gather | bytes 270336 | tf_op jit(solution)/shard_map/all_gather | solution.py:14
  85.9 24.2 %all-gather = f32[16384,4]{0,1:T(4,128)S(1)} all-gather(f32[512,4]{0,1:T(4,128)S(1)} %select_reduce_fusion.2), channel_id=2, replica_groups=mesh['pool'=32,'exp'=4] {'pool'}, dimensions={0}, use_global_device_ids=true | all-gather | bytes 270336 | tf_op jit(solution)/shard_map/all_gather | solution.py:14
  110.9 22.9 %all-gather.5.cloned.1.call-done = f32[16384,256]{1,0:T(8,128)} async-done(((f32[512,256]{1,0:T(8,128)}), f32[16384,256]{1,0:T(8,128)}) %all-gather.5.cloned.1.call-update) | async-done | bytes 16777232 | tf_op jit(solution)/shard_map/all_gather | solution.py:14
  135.0 11.4 %slice.35 = f32[15872,256]{1,0:T(8,128)} slice(f32[16384,256]{1,0:T(8,128)} %all-gather.5.cloned.1.call-done), slice={[512:16384], [0:256]} | slice | bytes 32505856 | tf_op jit(solution)/shard_map/slice | solution.py:16
  146.4 70.2 %while.14 = (s32[]{:T(128)}, f32[512,4]{0,1:T(4,128)S(1)}, f32[512,4]{0,1:T(4,128)S(1)}, f32[512,256]{0,1:T(8,128)S(1)}, f32[31,512,4]{1,2,0:T(4,128)}, /*index=...) while((s32[]{:T(128)}, f32[512,4]{0,1:T(4,128)S(1)}, f32[512,4]{0,1:T(4,128)S(1)}, ...), condition=%wide.region_8.9_spmd, body=%wide.region_7.8_spmd.sunk | while | flops 405506 | bytes 3752029 | solution.py:17
  147.2 1.1 constant_dynamic-slice_fusion.4
  149.4 1.1 constant_dynamic-slice_fusion.4
  151.7 1.1 constant_dynamic-slice_fusion.4
  153.9 1.1 constant_dynamic-slice_fusion.4
  156.2 1.1 constant_dynamic-slice_fusion.4
  158.5 1.1 constant_dynamic-slice_fusion.4
  160.7 1.1 constant_dynamic-slice_fusion.4
  163.0 1.1 constant_dynamic-slice_fusion.4
  165.3 1.1 constant_dynamic-slice_fusion.4
  167.5 1.1 constant_dynamic-slice_fusion.4
  169.8 1.1 constant_dynamic-slice_fusion.4
  172.1 1.1 constant_dynamic-slice_fusion.4
  174.3 1.1 constant_dynamic-slice_fusion.4
  176.6 1.1 constant_dynamic-slice_fusion.4
  178.8 1.1 constant_dynamic-slice_fusion.4
  181.1 1.1 constant_dynamic-slice_fusion.4
  183.4 1.1 constant_dynamic-slice_fusion.4
  185.6 1.1 constant_dynamic-slice_fusion.4
  187.9 1.1 constant_dynamic-slice_fusion.4
  190.2 1.1 constant_dynamic-slice_fusion.4
  192.4 1.1 constant_dynamic-slice_fusion.4
  194.7 1.1 constant_dynamic-slice_fusion.4
  199.2 1.1 constant_dynamic-slice_fusion.4
  201.5 1.1 constant_dynamic-slice_fusion.4
  210.5 1.1 constant_dynamic-slice_fusion.4
  217.8 37.8 %all-reduce.2.cloned.1.call-done = f32[16,1024]{1,0:T(8,128)} async-done(((f32[16,1024]{1,0:T(8,128)}), f32[16,1024]{1,0:T(8,128)}) %all-reduce.2.cloned.1.call-update) | async-done | bytes 65552 | tf_op jit(solution)/shard_map/psum | solution.py:141
  256.6 1.1 fusion.11
  257.7 9.7 %all-to-all-start.1 = ((bf16[32,8,1024]{2,1,0:T(8,128)(2,1)}), bf16[32,8,1024]{2,1,0:T(8,128)(2,1)S(1)}, u32[]{:S(2)}, u32[]{:S(2)}) async-start(bf16[32,8,1024]{2,1,0:T(8,128)(2,1)} %fusion.11), calls=%async_computation.1 | async-start | bytes 1048576 | tf_op jit(solution)/shard_map/all_to_all | solution.py:160
  267.5 11.5 %all-to-all-done.1 = bf16[32,8,1024]{2,1,0:T(8,128)(2,1)S(1)} async-done(((bf16[32,8,1024]{2,1,0:T(8,128)(2,1)}), bf16[32,8,1024]{2,1,0:T(8,128)(2,1)S(1)}, u32[]{:S(2)}, u32[]{:S(2)}) %all-to-all-start.1) | async-done | bytes 524320 | tf_op jit(solution)/shard_map/all_to_all | solution.py:160
  279.0 1.7 fusion.20
  280.7 2.0 fusion.12
  283.4 3.6 %all-to-all-start.2 = ((bf16[32,8,256]{2,1,0:T(8,128)(2,1)}), bf16[32,8,256]{2,1,0:T(8,128)(2,1)S(1)}, u32[]{:S(2)}, u32[]{:S(2)}) async-start(bf16[32,8,256]{2,1,0:T(8,128)(2,1)} %constant_dynamic-slice_fusion.2), calls=%async_computation.2 | async-start | bytes 262144 | tf_op jit(solution)/shard_map/all_to_all | solution.py:170
  287.3 7.4 %all-to-all-done.2 = bf16[32,8,256]{2,1,0:T(8,128)(2,1)S(1)} async-done(((bf16[32,8,256]{2,1,0:T(8,128)(2,1)}), bf16[32,8,256]{2,1,0:T(8,128)(2,1)S(1)}, u32[]{:S(2)}, u32[]{:S(2)}) %all-to-all-start.2) | async-done | bytes 131104 | tf_op jit(solution)/shard_map/all_to_all | solution.py:170
  (175 shorter events, 57.3 us)
Async XLA Ops:
  6.5 274.1 %copy-start = (bf16[1,512,1024]{2,1,0:T(8,128)(2,1)S(1)}, bf16[1,512,1024]{2,1,0:T(8,128)(2,1)}, u32[]{:S(2)}) copy-start(bf16[1,512,1024]{2,1,0:T(8,128)(2,1)} %param.35) | copy-start | bytes 3145732
  6.5 23.4 %copy-start.8 = (bf16[1024,128]{1,0:T(8,128)(2,1)S(1)}, bf16[1024,128]{1,0:T(8,128)(2,1)}, u32[]{:S(2)}) copy-start(bf16[1024,128]{1,0:T(8,128)(2,1)} %param.28) | copy-start | bytes 786436
  10.2 36.6 %all-to-all-start = ((bf16[32,16,256]{2,1,0:T(8,128)(2,1)}), bf16[32,16,256]{2,1,0:T(8,128)(2,1)S(1)}, u32[]{:S(2)}, u32[]{:S(2)}) async-start(bf16[32,16,256]{2,1,0:T(8,128)(2,1)} %stack.2), calls=%async_computation | async-start | bytes 524288 | tf_op jit(solution)/shard_map/all_to_all | solution.py:69
  19.7 114.0 %all-gather.5.cloned.1.call-start = ((), (), s32[]{:S(2)}) async-start(), calls=%async_computation.4 | async-start | bytes 17301504 | tf_op jit(solution)/shard_map/all_gather | solution.py:14
  19.7 10.2 %copy-start.7 = (bf16[16,128,1024]{2,1,0:T(8,128)(2,1)S(1)}, bf16[16,128,1024]{2,1,0:T(8,128)(2,1)}, u32[]{:S(2)}) copy-start(bf16[16,128,1024]{2,1,0:T(8,128)(2,1)} %param.24) | copy-start | bytes 12582916
  30.0 1.3 copy-start.6
  52.1 6.7 %copy-start.3 = (s32[16,8]{0,1:T(8,128)S(1)}, s32[16,8]{0,1:T(8,128)}, u32[]{:S(2)}) copy-start(s32[16,8]{0,1:T(8,128)} %param.31) | copy-start | bytes 1540
  52.1 7.4 %copy-start.5 = (bf16[1024]{0:T(1024)(128)(2,1)S(1)}, bf16[1024]{0:T(1024)(128)(2,1)}, u32[]{:S(2)}) copy-start(bf16[1024]{0:T(1024)(128)(2,1)} %param.30) | copy-start | bytes 6148
  58.7 196.9 %all-reduce.2.cloned.1.call-start = ((), (), s32[]{:S(2)}) async-start(), calls=%async_computation.3 | async-start | bytes 131072 | tf_op jit(solution)/shard_map/psum | solution.py:141
  146.4 70.4 %copy-start.1 = (bf16[256,1024]{1,0:T(8,128)(2,1)S(1)}, bf16[256,1024]{1,0:T(8,128)(2,1)}, u32[]{:S(2)}) copy-start(bf16[256,1024]{1,0:T(8,128)(2,1)} %param.29) | copy-start | bytes 1572868
  146.4 109.2 %copy-start.2 = (bf16[16,1024]{1,0:T(8,128)(2,1)S(1)}, bf16[16,1024]{1,0:T(8,128)(2,1)}, u32[]{:S(2)}) copy-start(bf16[16,1024]{1,0:T(8,128)(2,1)} %param.19) | copy-start | bytes 98308
  146.4 121.0 %copy-start.4 = (f32[16,8]{0,1:T(8,128)S(1)}, f32[16,8]{0,1:T(8,128)}, u32[]{:S(2)}) copy-start(f32[16,8]{0,1:T(8,128)} %param.32) | copy-start | bytes 1540
  257.7 21.3 %all-to-all-start.1 = ((bf16[32,8,1024]{2,1,0:T(8,128)(2,1)}), bf16[32,8,1024]{2,1,0:T(8,128)(2,1)S(1)}, u32[]{:S(2)}, u32[]{:S(2)}) async-start(bf16[32,8,1024]{2,1,0:T(8,128)(2,1)} %fusion.11), calls=%async_computation.1 | async-start | bytes 1048576 | tf_op jit(solution)/shard_map/all_to_all | solution.py:160
  283.4 11.3 %all-to-all-start.2 = ((bf16[32,8,256]{2,1,0:T(8,128)(2,1)}), bf16[32,8,256]{2,1,0:T(8,128)(2,1)S(1)}, u32[]{:S(2)}, u32[]{:S(2)}) async-start(bf16[32,8,256]{2,1,0:T(8,128)(2,1)} %constant_dynamic-slice_fusion.2), calls=%async_computation.2 | async-start | bytes 262144 | tf_op jit(solution)/shard_map/all_to_all | solution.py:170
Sparse Core Ops, SparseCore 0:
  58.8 74.8 all-gather.4
  217.8 37.7 all-reduce.1
